TPU v7x, 256 devices: a whole 4x4x8 slice. The times are simulated.
256 devices in a mesh: band: 4 (over z_hi, core), grid: 64 (over y, z_lo, x).
Axes of the slice: x: 4, y: 4, z: 8 (z_hi: 2, z_lo: 4; z = z_hi * 4 + z_lo), core: 2. Of those that a mesh axis runs over, the one named last changes fastest.
Arguments:
- orbitals: bfloat16 [256, 384, 32, 128], P('band', 'grid'), may hold values from -24 to 24, as said below
- potential: float32 [384, 32, 128], P('grid'), may hold values from -1 to 1
Outputs:
- gradient: float32 [256, 384, 32, 128], P('band', 'grid')
- intersection: float32 [256, 256], P('band')
- subspace: float32 [256, 256], P('band')
Inputs may be any that keep to these rules, and one draw needn't show every extreme that they name: `orbitals`: orbital values of order one.
All inputs are finite; a program needn't handle non-finite values.
Results may differ from a plain program's by a relative error of at most 0.0003.
Values may be sent and summed in bfloat16 or wider, within the bound.
A program may use at most 128 MiB of HBM per device.

v0:
```python
import jax
import jax.numpy as jnp
from jax import lax
from jax.sharding import PartitionSpec as P

COEFFS = (-49.0 / 18.0, 3.0 / 2.0, -3.0 / 20.0, 1.0 / 90.0)


def padded_2(cells, sides, width):
    for axis, dim in sides:
        count = lax.axis_size(axis)
        head = lax.slice_in_dim(cells, 0, width, axis=dim)
        tail = lax.slice_in_dim(cells, cells.shape[dim] - width, cells.shape[dim], axis=dim)
        cells = jnp.concatenate(
            [
                lax.ppermute(tail, axis, [(i, (i + 1) % count) for i in range(count)]),
                cells,
                lax.ppermute(head, axis, [((i + 1) % count, i) for i in range(count)]),
            ],
            axis=dim,
        )
    return cells


def apply_hamiltonian(padded, potential):
    stencil_reach = len(COEFFS) - 1
    width_x = padded.shape[1] - 2 * stencil_reach
    planes = padded.shape[2]
    center = padded[:, stencil_reach : stencil_reach + width_x].astype(jnp.float32)
    z_padded = jnp.pad(center, ((0, 0), (0, 0), (stencil_reach, stencil_reach), (0, 0)))
    total = 3.0 * COEFFS[0] * center
    for shift_by in range(1, stencil_reach + 1):
        pair_x = padded[:, stencil_reach + shift_by : stencil_reach + shift_by + width_x].astype(
            jnp.float32
        ) + padded[:, stencil_reach - shift_by : stencil_reach - shift_by + width_x].astype(
            jnp.float32
        )
        pair_z = (
            z_padded[:, :, stencil_reach + shift_by : stencil_reach + shift_by + planes]
            + z_padded[:, :, stencil_reach - shift_by : stencil_reach - shift_by + planes]
        )
        pair_y = jnp.roll(center, shift_by, 3) + jnp.roll(center, -shift_by, 3)
        total = total + COEFFS[shift_by] * (pair_x + pair_z + pair_y)
    return -0.5 * total + potential * center


def row_products(left, right):
    return lax.dot_general(
        left, right, (((1,), (1,)), ((), ())), preferred_element_type=jnp.float32
    )


def body(orbitals, potential):
    shape = orbitals.shape
    orb_dev = shape[0]
    cell_count = shape[1] * lax.axis_size("grid") * shape[2] * shape[3]
    group_count = orb_dev // 16
    stencil_reach = len(COEFFS) - 1
    padded = padded_2(orbitals, (("grid", 1),), stencil_reach)
    groups = padded.reshape((group_count, 16) + padded.shape[1:])
    hpsi = lax.map(lambda group: apply_hamiltonian(group, potential), groups).reshape(shape)
    flat_psi = orbitals.reshape(orb_dev, -1)
    flat_h = hpsi.astype(jnp.bfloat16).reshape(orb_dev, -1)
    panel_rows = lax.all_gather(flat_psi, "band", axis=0, tiled=True)
    s_rows = row_products(flat_psi, panel_rows)
    h_rows = row_products(flat_h, panel_rows)
    s_rows, h_rows = (s_rows, h_rows)
    s_summed, h_summed = lax.psum((s_rows, h_rows), "grid")
    intersection = s_summed / cell_count
    subspace = h_summed / cell_count
    offset_rows = lax.axis_index("band") * orb_dev
    s_diag = jnp.diagonal(lax.dynamic_slice_in_dim(intersection, offset_rows, orb_dev, 1))
    h_diag = jnp.diagonal(lax.dynamic_slice_in_dim(subspace, offset_rows, orb_dev, 1))
    rayleigh = h_diag / (s_diag + 1e-06)
    gradient = (hpsi - rayleigh[:, None, None, None] * orbitals.astype(jnp.float32)) / (
        2.0 + potential
    )
    return (gradient, intersection, subspace)


def solution(mesh):
    in_specs = (P("band", "grid", None, None), P("grid", None, None))
    out_specs = (P("band", "grid", None, None), P("band", None), P("band", None))
    return jax.shard_map(body, mesh=mesh, in_specs=in_specs, out_specs=out_specs, check_vma=False)
```

profile of v0, /device:TPU:2, one launch (start us, length us, event | category | flops | bytes accessed | tf_op | source)
XLA Modules:
  0.0 889.9 jit_solution(4659854884611012534)
XLA Ops:
  7.2 0.0 all-gather.2.cloned.1.call-start
  7.2 5.6 copy.8
  12.8 0.0 all-gather.2.cloned.1.call-update
  12.9 0.0 all-reduce.4.cloned.1.call-start
  12.9 1.8 copy-done
  14.7 2.3 fusion.27
  17.0 1.5 collective-permute-start
  18.5 0.8 collective-permute-start.1
  19.2 34.2 %collective-permute-done = bf16[64,3,32,128]{3,2,1,0:T(8,128)(2,1)} collective-permute-done((bf16[64,3,32,128]{3,2,1,0:T(8,128)(2,1)}, bf16[64,3,32,128]{3,2,1,0:T(8,128)(2,1)}, u32[]{:S(2)}, u32[]{:S(2)}) %collective-permute-start) | collective-permute-done | bytes 1572896 | tf_op jit(solution)/shard_map/ppermute | solution.py:16
  53.4 1.2 collective-permute-done.1
  54.6 5.0 pad_maximum_fusion
  59.6 59.5 %while.12 = (s32[]{:T(128)}, f32[4,16,6,32,128]{4,3,2,1,0:T(8,128)}, bf16[4,16,12,32,128]{4,3,2,1,0:T(8,128)(2,1)}, f32[6,32,128]{2,1,0:T(8,128)S(1)}, s32[]{:T(128)}) while((s32[]{:T(128)}, f32[4,16,6,32,128]{4,3,2,1,0:T(8,128)}, bf16[4,16,12,32,128]{4,3,2,1,0:T(8,128)(2,1)}, f32[6,32,128]{2,1,0:T(8,128)S(1)}, s32[]{:T(128)}) %tuple.59), condition=%wide.region_1.2_spmd, body=%wide.region_0.1_spmd.sunk | while | flops 14942210 | bytes 44888640 | solution.py:61
  59.6 1.7 dynamic-slice_bitcast_fusion.2
  61.3 0.2 slice_convert_fusion.2
  61.5 0.6 fusion.39
  62.1 0.6 fusion.40
  62.7 0.6 fusion.41
  63.3 0.6 fusion.42
  63.9 1.7 fusion.43
  65.6 2.3 fusion.44
  67.9 6.6 fusion.45
  74.5 1.7 dynamic-slice_bitcast_fusion.2
  76.2 0.2 slice_convert_fusion.2
  76.4 0.6 fusion.39
  77.0 0.6 fusion.40
  77.6 0.6 fusion.41
  78.2 0.6 fusion.42
  78.8 1.7 fusion.43
  80.5 2.3 fusion.44
  82.8 6.6 fusion.45
  89.4 1.7 dynamic-slice_bitcast_fusion.2
  91.1 0.2 slice_convert_fusion.2
  91.3 0.6 fusion.39
  91.9 0.6 fusion.40
  92.5 0.6 fusion.41
  93.1 0.6 fusion.42
  93.7 1.7 fusion.43
  95.4 2.2 fusion.44
  97.6 6.8 fusion.45
  104.4 1.7 dynamic-slice_bitcast_fusion.2
  106.1 0.2 slice_convert_fusion.2
  106.3 0.6 fusion.39
  106.9 0.6 fusion.40
  107.5 0.6 fusion.41
  108.0 0.6 fusion.42
  108.6 1.7 fusion.43
  110.4 2.2 fusion.44
  112.6 6.6 fusion.45
  119.2 5.3 convert_element_type.56
  124.5 5.0 convert_element_type.57
  129.5 46.6 %all-gather.2.cloned.1.call-done = bf16[256,24576]{1,0:T(8,128)(2,1)} async-done(((bf16[64,24576]{1,0:T(8,128)(2,1)}), bf16[256,24576]{1,0:T(8,128)(2,1)}) %all-gather.2.cloned.1.call-update) | async-done | bytes 12582928 | tf_op jit(solution)/shard_map/all_gather | solution.py:64
  176.2 0.0 copy-done.1
  176.2 9.3 %fusion.20 = f32[64,256]{1,0:T(8,128)} fusion(bf16[256,24576]{1,0:T(8,128)(2,1)} %all-gather.2.cloned.1.call-done, bf16[8,8,192,128]{3,2,1,0:T(8,128)(2,1)S(1)} %bitcast.29), kind=kOutput, calls=%fused_computation.43 | convolution fusion | flops 805306368 | bytes 15794176 | tf_op jit(solution)/shard_map/dot_general | solution.py:48
  185.5 9.1 %fusion.28 = f32[64,256]{1,0:T(8,128)} fusion(bf16[64,24576]{1,0:T(8,128)(2,1)S(1)} %copy-done.2, bf16[256,24576]{1,0:T(8,128)(2,1)} %all-gather.2.cloned.1.call-done), kind=kOutput, calls=%fused_computation.51 | convolution fusion | flops 805306368 | bytes 15794176 | tf_op jit(solution)/shard_map/dot_general | solution.py:48
  194.6 0.0 all-reduce.4.cloned.1.call-update
  194.6 678.5 %all-reduce.4.cloned.1.call-done = (f32[64,256]{1,0:T(8,128)}, f32[64,256]{1,0:T(8,128)}) async-done(((f32[64,256]{1,0:T(8,128)}, f32[64,256]{1,0:T(8,128)}), (f32[64,256]{1,0:T(8,128)}, f32[64,256]{1,0:T(8,128)})) %all-reduce.4.cloned.1.call-update) | async-done | bytes 131088 | tf_op jit(solution)/shard_map/psum | solution.py:68
  873.1 0.9 broadcast_multiply_fusion
  874.0 0.0 copy-start.4
  874.0 0.0 copy-start.5
  874.0 0.1 constant_dynamic-slice_fusion
  874.1 0.1 constant_dynamic-slice_fusion.1
  874.2 0.8 gather_fusion.1
  875.0 0.8 gather_fusion
  875.8 7.2 fusion.19
  (12 shorter events, 0.0 us)
Async XLA Ops:
  7.2 169.0 %all-gather.2.cloned.1.call-start = ((), (), s32[]{:S(2)}) async-start(), calls=%async_computation | async-start | bytes 15728640 | tf_op jit(solution)/shard_map/all_gather | solution.py:64
  12.8 1.9 copy-start
  12.9 860.3 %all-reduce.4.cloned.1.call-start = ((), (), s32[]{:S(2)}) async-start(), calls=%async_computation.1 | async-start | bytes 262144 | tf_op jit(solution)/shard_map/psum | solution.py:68
  17.0 36.5 %collective-permute-start = (bf16[64,3,32,128]{3,2,1,0:T(8,128)(2,1)}, bf16[64,3,32,128]{3,2,1,0:T(8,128)(2,1)}, u32[]{:S(2)}, u32[]{:S(2)}) collective-permute-start(bf16[64,3,32,128]{3,2,1,0:T(8,128)(2,1)} %get-tuple-element.79), channel_id=1, source_target_pairs={{0,1},{1,2},{2,3},{3,4},{4,5},{5,6},{6,7},{7,8},{8,9},{9,10},{10,1... | collective-permute-start | bytes 4718600 | tf_op jit(solution)/shard_map/ppermute | solution.py:16
  18.5 36.2 %collective-permute-start.1 = (bf16[64,3,32,128]{3,2,1,0:T(8,128)(2,1)}, bf16[64,3,32,128]{3,2,1,0:T(8,128)(2,1)}, u32[]{:S(2)}, u32[]{:S(2)}) collective-permute-start(bf16[64,3,32,128]{3,2,1,0:T(8,128)(2,1)} %get-tuple-element.80), channel_id=1, source_target_pairs={{1,0},{2,1},{3,2},{4,3},{5,4},{6,5},{7,6},{8,7},{9,8},{10,9},{11,1... | collective-permute-start | bytes 4718600 | tf_op jit(solution)/shard_map/ppermute | solution.py:18
  19.2 40.4 %copy-start.3 = (f32[6,32,128]{2,1,0:T(8,128)S(1)}, f32[6,32,128]{2,1,0:T(8,128)}, u32[]{:S(2)}) copy-start(f32[6,32,128]{2,1,0:T(8,128)} %param.5) | copy-start | bytes 294916
  124.5 51.6 %copy-start.1 = (bf16[64,6,32,128]{3,2,1,0:T(8,128)(2,1)S(1)}, bf16[64,6,32,128]{3,2,1,0:T(8,128)(2,1)}, u32[]{:S(2)}) copy-start(bf16[64,6,32,128]{3,2,1,0:T(8,128)(2,1)} %param.4) | copy-start | bytes 9437188
  176.2 9.3 %copy-start.2 = (bf16[64,24576]{1,0:T(8,128)(2,1)S(1)}, bf16[64,24576]{1,0:T(8,128)(2,1)}, u32[]{:S(2)}) copy-start(bf16[64,24576]{1,0:T(8,128)(2,1)} %convert_element_type.57) | copy-start | bytes 9437188
  874.0 9.0 %copy-start.4 = (f32[64,256]{1,0:T(8,128)}, f32[64,256]{1,0:T(8,128)S(1)}, u32[]{:S(2)}) copy-start(f32[64,256]{1,0:T(8,128)S(1)} %get-tuple-element.81) | copy-start | bytes 196612
  874.0 9.0 %copy-start.5 = (f32[64,256]{1,0:T(8,128)}, f32[64,256]{1,0:T(8,128)S(1)}, u32[]{:S(2)}) copy-start(f32[64,256]{1,0:T(8,128)S(1)} %get-tuple-element.82) | copy-start | bytes 196612
Sparse Core Ops, SparseCore 0:
  13.0 163.1 all-gather.1
  194.7 678.3 all-reduce.3
where the time goes:
time: 890 us
  waiting for transfers between devices  761 us (86%)
  local copies, waits for them, and re-layouts  48.4 us (5%)
  other arithmetic  45.8 us (5%)
  matrix products  18.4 us (2%)
  between operations  14.1 us (2%)
    psum x1, waiting for transfers between devices, body(): s_summed, h_summed = lax.psum((s_rows, h_rows), 'grid')  678 us
    all_gather x1, waiting for transfers between devices, body(): panel_rows = lax.all_gather(flat_psi, 'band', axis=0, tiled=True)  46.6 us
    ppermute x1, waiting for transfers between devices, padded_2(): lax.ppermute(tail, axis, [(i, (i + 1) % count) for i in range(count)])  34.2 us
    dynamic_update_slice x4, other arithmetic, body(): lax.map(lambda group: apply_hamiltonian(group, potential), groups)  26.6 us
    slice x24, local copies, waits for them, and re-layouts, apply_hamiltonian(): pair_y = jnp.roll(center, shift_by, 3) + jnp.roll(center, -shift_by, 3)  25.2 us
    dot_general x2, matrix products, row_products(): lax.dot_general(left, right, (((1,), (1,)), ((), ())), preferred_element_...  18.4 us
  transfers between devices with their start and end apart: 4, of which 4 were waited for; matrix products, arithmetic and copies ran while one was open for 9% of the time, Pallas kernels for 0%

commit v1 on v0

--- a/solution.py
+++ b/solution.py
@@ -61,7 +61,9 @@
     hpsi = lax.map(lambda group: apply_hamiltonian(group, potential), groups).reshape(shape)
     flat_psi = orbitals.reshape(orb_dev, -1)
     flat_h = hpsi.astype(jnp.bfloat16).reshape(orb_dev, -1)
-    panel_rows = lax.all_gather(flat_psi, "band", axis=0, tiled=True)
+    panel_rows = jnp.concatenate(
+        lax.all_to_all(jnp.stack([flat_psi] * lax.axis_size("band")), "band", 0, 0), axis=0
+    )
     s_rows = row_products(flat_psi, panel_rows)
     h_rows = row_products(flat_h, panel_rows)
     s_rows, h_rows = (s_rows, h_rows)

time: 890 us -> 1080 us (1.21)
  waiting for transfers between devices: 761 us -> 941 us
    all_to_all x0 -> x1, waiting for transfers between devices: none -> 163 us  [body(): lax.all_to_all(jnp.stack([flat_psi] * lax.axis_size('band')), 'band', 0, 0)]
    psum x1, waiting for transfers between devices: 678 us -> 742 us  [body(): s_summed, h_summed = lax.psum((s_rows, h_rows), 'grid')]
    all_gather x1 -> x0, waiting for transfers between devices: 46.6 us -> none  [body(): panel_rows = lax.all_gather(flat_psi, 'band', axis=0, tiled=True)]
  transfers between devices with their start and end apart: 4 -> 4, of which waited for: 4 -> 4; matrix products, arithmetic and copies ran while one was open for 9% -> 7% of each run, Pallas kernels for 0% -> 0%
where the time goes in v1:
time: 1080 us
  waiting for transfers between devices  941 us (87%)
  local copies, waits for them, and re-layouts  51.1 us (5%)
  other arithmetic  45.8 us (4%)
  matrix products  18.4 us (2%)
  between operations  14.1 us (1%)
    psum x1, waiting for transfers between devices, body(): s_summed, h_summed = lax.psum((s_rows, h_rows), 'grid')  742 us
    all_to_all x1, waiting for transfers between devices, body(): lax.all_to_all(jnp.stack([flat_psi] * lax.axis_size('band')), 'band', 0, 0)  163 us
    ppermute x1, waiting for transfers between devices, padded_2(): lax.ppermute(tail, axis, [(i, (i + 1) % count) for i in range(count)])  35.1 us
    dynamic_update_slice x4, other arithmetic, body(): lax.map(lambda group: apply_hamiltonian(group, potential), groups)  26.6 us
    slice x24, local copies, waits for them, and re-layouts, apply_hamiltonian(): pair_y = jnp.roll(center, shift_by, 3) + jnp.roll(center, -shift_by, 3)  25 us
  transfers between devices with their start and end apart: 4, of which 4 were waited for; matrix products, arithmetic and copies ran while one was open for 7% of the time, Pallas kernels for 0%

profile of v1, /device:TPU:2, one launch (start us, length us, event | category | flops | bytes accessed | tf_op | source)
XLA Modules:
  0.0 1081.5 jit_solution(5646459006486532567)
XLA Ops:
  7.2 3.9 copy.8
  11.1 6.1 stack.3
  17.2 8.7 all-to-all-start
  26.0 0.0 all-reduce.4.cloned.1.call-start
  26.0 0.0 copy-done
  26.0 2.2 fusion.27
  28.2 1.5 collective-permute-start
  29.7 0.5 collective-permute-start.1
  30.2 35.1 %collective-permute-done = bf16[64,3,32,128]{3,2,1,0:T(8,128)(2,1)} collective-permute-done((bf16[64,3,32,128]{3,2,1,0:T(8,128)(2,1)}, bf16[64,3,32,128]{3,2,1,0:T(8,128)(2,1)}, u32[]{:S(2)}, u32[]{:S(2)}) %collective-permute-start) | collective-permute-done | bytes 1572896 | tf_op jit(solution)/shard_map/ppermute | solution.py:16
  65.3 1.2 collective-permute-done.1
  66.5 5.0 pad_maximum_fusion
  71.5 59.6 %while.12 = (s32[]{:T(128)}, f32[4,16,6,32,128]{4,3,2,1,0:T(8,128)}, bf16[4,16,12,32,128]{4,3,2,1,0:T(8,128)(2,1)}, f32[6,32,128]{2,1,0:T(8,128)S(1)}, s32[]{:T(128)}) while((s32[]{:T(128)}, f32[4,16,6,32,128]{4,3,2,1,0:T(8,128)}, bf16[4,16,12,32,128]{4,3,2,1,0:T(8,128)(2,1)}, f32[6,32,128]{2,1,0:T(8,128)S(1)}, s32[]{:T(128)}) %tuple.57), condition=%wide.region_1.2_spmd, body=%wide.region_0.1_spmd.sunk | while | flops 14942210 | bytes 44888640 | solution.py:61
  71.5 1.7 dynamic-slice_bitcast_fusion.2
  73.3 0.2 slice_convert_fusion.2
  73.5 0.6 fusion.39
  74.1 0.6 fusion.40
  74.7 0.6 fusion.41
  75.2 0.6 fusion.42
  75.8 1.8 fusion.43
  77.6 2.2 fusion.44
  79.8 6.6 fusion.45
  86.4 1.7 dynamic-slice_bitcast_fusion.2
  88.2 0.2 slice_convert_fusion.2
  88.4 0.6 fusion.39
  89.0 0.6 fusion.40
  89.5 0.6 fusion.41
  90.1 0.6 fusion.42
  90.7 1.8 fusion.43
  92.4 2.2 fusion.44
  94.7 6.6 fusion.45
  101.3 1.7 dynamic-slice_bitcast_fusion.2
  103.0 0.2 slice_convert_fusion.2
  103.2 0.6 fusion.39
  103.8 0.6 fusion.40
  104.4 0.6 fusion.41
  105.0 0.6 fusion.42
  105.6 1.8 fusion.43
  107.3 2.2 fusion.44
  109.5 6.7 fusion.45
  116.2 1.7 dynamic-slice_bitcast_fusion.2
  118.0 0.2 slice_convert_fusion.2
  118.2 0.6 fusion.39
  118.8 0.6 fusion.40
  119.3 0.6 fusion.41
  119.9 0.6 fusion.42
  120.5 1.8 fusion.43
  122.3 2.2 fusion.44
  124.5 6.6 fusion.45
  131.1 5.3 convert_element_type.56
  136.4 5.0 convert_element_type.57
  141.4 162.7 %all-to-all-done = bf16[4,64,24576]{2,1,0:T(8,128)(2,1)} async-done(((bf16[4,64,24576]{2,1,0:T(8,128)(2,1)}), bf16[4,64,24576]{2,1,0:T(8,128)(2,1)}, u32[]{:S(2)}, u32[]{:S(2)}) %all-to-all-start) | async-done | bytes 12582944 | tf_op jit(solution)/shard_map/all_to_all | solution.py:65
  304.1 9.3 fusion.20
  313.4 9.1 fusion.28
  322.5 0.0 all-reduce.4.cloned.1.call-update
  322.5 742.2 %all-reduce.4.cloned.1.call-done = (f32[64,256]{1,0:T(8,128)}, f32[64,256]{1,0:T(8,128)}) async-done(((f32[64,256]{1,0:T(8,128)}, f32[64,256]{1,0:T(8,128)}), (f32[64,256]{1,0:T(8,128)}, f32[64,256]{1,0:T(8,128)})) %all-reduce.4.cloned.1.call-update) | async-done | bytes 131088 | tf_op jit(solution)/shard_map/psum | solution.py:70
  1064.7 0.9 broadcast_multiply_fusion
  1065.6 0.0 copy-start.4
  1065.6 0.0 copy-start.5
  1065.6 0.1 constant_dynamic-slice_fusion
  1065.7 0.1 constant_dynamic-slice_fusion.1
  1065.8 0.8 gather_fusion.1
  1066.6 0.8 gather_fusion
  1067.4 7.2 fusion.19
  1074.6 0.0 copy-done.4
  (12 shorter events, 0.0 us)
Async XLA Ops:
  17.2 8.7 copy-start
  17.2 286.8 %all-to-all-start = ((bf16[4,64,24576]{2,1,0:T(8,128)(2,1)}), bf16[4,64,24576]{2,1,0:T(8,128)(2,1)}, u32[]{:S(2)}, u32[]{:S(2)}) async-start(bf16[4,64,24576]{2,1,0:T(8,128)(2,1)} %stack.3), calls=%async_computation | async-start | bytes 25165824 | tf_op jit(solution)/shard_map/all_to_all | solution.py:65
  26.0 1038.7 %all-reduce.4.cloned.1.call-start = ((), (), s32[]{:S(2)}) async-start(), calls=%async_computation.1 | async-start | bytes 262144 | tf_op jit(solution)/shard_map/psum | solution.py:70
  28.2 37.1 %collective-permute-start = (bf16[64,3,32,128]{3,2,1,0:T(8,128)(2,1)}, bf16[64,3,32,128]{3,2,1,0:T(8,128)(2,1)}, u32[]{:S(2)}, u32[]{:S(2)}) collective-permute-start(bf16[64,3,32,128]{3,2,1,0:T(8,128)(2,1)} %get-tuple-element.79), channel_id=1, source_target_pairs={{0,1},{1,2},{2,3},{3,4},{4,5},{5,6},{6,7},{7,8},{8,9},{9,10},{10,1... | collective-permute-start | bytes 4718600 | tf_op jit(solution)/shard_map/ppermute | solution.py:16
  29.7 36.8 %collective-permute-start.1 = (bf16[64,3,32,128]{3,2,1,0:T(8,128)(2,1)}, bf16[64,3,32,128]{3,2,1,0:T(8,128)(2,1)}, u32[]{:S(2)}, u32[]{:S(2)}) collective-permute-start(bf16[64,3,32,128]{3,2,1,0:T(8,128)(2,1)} %get-tuple-element.80), channel_id=1, source_target_pairs={{1,0},{2,1},{3,2},{4,3},{5,4},{6,5},{7,6},{8,7},{9,8},{10,9},{11,1... | collective-permute-start | bytes 4718600 | tf_op jit(solution)/shard_map/ppermute | solution.py:18
  30.2 41.3 %copy-start.3 = (f32[6,32,128]{2,1,0:T(8,128)S(1)}, f32[6,32,128]{2,1,0:T(8,128)}, u32[]{:S(2)}) copy-start(f32[6,32,128]{2,1,0:T(8,128)} %param.5) | copy-start | bytes 294916
  136.4 167.6 %copy-start.1 = (bf16[64,6,32,128]{3,2,1,0:T(8,128)(2,1)S(1)}, bf16[64,6,32,128]{3,2,1,0:T(8,128)(2,1)}, u32[]{:S(2)}) copy-start(bf16[64,6,32,128]{3,2,1,0:T(8,128)(2,1)} %param.4) | copy-start | bytes 9437188
  304.1 9.3 copy-start.2
  1065.6 9.0 copy-start.4
  1065.6 9.0 copy-start.5
Sparse Core Ops, SparseCore 0:
  322.6 742.0 all-reduce.3
